TPU v7x, 32 devices: a whole 2x2x4 slice. The times are simulated.
32 devices in a mesh: tm: 2 (over x), cell: 16 (over z, y, core).
Axes of the slice: x: 2, y: 2, z: 4, core: 2. Of those that a mesh axis runs over, the one named last changes fastest.
Arguments:
- initial: float32 [4096, 128], P('cell'), may hold values from 0.2 to 6, as said below
- source: float32 [4, 4096, 128], P('tm', 'cell'), may hold values from -1.8 to 1.8
- mix_rate: float32 [128], replicated, may hold values from 0.05 to 0.4
- fine_inverse: float32 [4, 32, 128, 128], P('tm', 'cell'), may hold values from -0.1 to 0.9, as said below
- coarse_inverse: float32 [4, 32, 128, 128], P('tm', 'cell'), may hold values from -0.1 to 1, as said below
- step_counts: int32 [4096], P('cell'), may hold values from 4 to 8
Outputs:
- finals: float32 [4, 4096, 128], P('tm', 'cell')
Inputs may be any that keep to these rules, and one draw needn't show every extreme that they name: `initial`: positive compositions. `fine_inverse`: each matrix is a positive diagonal plus small off-diagonal entries. `coarse_inverse`: each matrix is a positive diagonal plus small off-diagonal entries.
All inputs are finite; a program needn't handle non-finite values.
Results may differ from a plain program's by a relative error of at most 0.00011.
Values sent between devices are 32-bit elements; how exact they have to be, the bound alone decides.
No kernel may reach another device: no remote copies, remote signals or barrier semaphores. Data moves between devices by JAX's collectives and lax.ppermute only.
A program may use at most 64 MiB of HBM per device.

v0:
```python
import jax
import jax.numpy as jnp
from jax import lax
from jax.sharding import PartitionSpec as P

FINE_MAX = 8
ITERS = 2


def from_behind(block, axis, distance):
    devices = range(lax.axis_size(axis))
    route = [(i - distance, i) for i in devices if i - distance in devices]
    return lax.ppermute(block, axis, route)


def group_mul(state, matrices):
    count, width = state.shape
    groups = matrices.shape[0]
    shaped = state.reshape(groups, count // groups, width)
    result = jnp.einsum("gcs,gst->gct", shaped, matrices, precision=lax.Precision.HIGHEST)
    return result.reshape(count, width)


def slices_mul(state, matrices):
    lead, count, width = state.shape
    groups = matrices.shape[1]
    shaped = state.reshape(lead, groups, count // groups, width)
    result = jnp.einsum("lgcs,lgst->lgct", shaped, matrices, precision=lax.Precision.HIGHEST)
    return result.reshape(lead, count, width)


def local_chain(incoming, offsets, coarse_inverse):
    state = incoming
    results = []
    for index in range(offsets.shape[0]):
        state = group_mul(state, coarse_inverse[index]) + offsets[index]
        results.append(state)
    return jnp.stack(results, axis=0)


def zero_start_end(offsets, coarse_inverse):
    state = offsets[0]
    state = group_mul(state, coarse_inverse[1]) + offsets[1]
    return state


def across(initial, offsets, coarse_inverse):
    composed = coarse_inverse[0]
    composed = jnp.einsum(
        "gst,gtu->gsu", composed, coarse_inverse[1], precision=lax.Precision.HIGHEST
    )
    shifted = zero_start_end(offsets, coarse_inverse)
    leading = lax.axis_index("tm") == 0

    def advance(turn, incoming):
        ending = group_mul(incoming, composed) + shifted
        received = from_behind(ending, "tm", 1)
        return jnp.where(leading, initial, received)

    incoming = lax.fori_loop(0, lax.axis_size("tm") - 1, advance, initial)
    return (incoming, local_chain(incoming, offsets, coarse_inverse))


def body(initial, source, mix_rate, fine_inverse, coarse_inverse, step_counts):
    total = initial.shape[0] * lax.axis_size("cell")
    offsets0 = slices_mul(source, coarse_inverse)
    incoming, finals = across(initial, offsets0, coarse_inverse)
    for sweep_round in range(ITERS):
        starts = jnp.concatenate([incoming[None], finals[:-1]], axis=0)
        state = starts
        for substep in range(FINE_MAX):
            average = lax.psum(jnp.sum(state, axis=1), "cell") / total
            moved = slices_mul(
                state + source + mix_rate * (average[:, None, :] - state), fine_inverse
            )
            active = (substep < step_counts)[None, :, None]
            state = jnp.where(active, moved, state)
        coarse_ends = slices_mul(starts, coarse_inverse) + offsets0
        offsets = offsets0 + state - coarse_ends
        incoming, finals = across(initial, offsets, coarse_inverse)
    return finals


def solution(mesh):
    return jax.shard_map(
        body,
        mesh=mesh,
        in_specs=(
            P("cell", None),
            P("tm", "cell", None),
            P(),
            P("tm", "cell", None, None),
            P("tm", "cell", None, None),
            P("cell"),
        ),
        out_specs=P("tm", "cell", None),
        check_vma=False,
    )
```

profile of v0, /device:TPU:0, one launch (start us, length us, event | category | flops | bytes accessed | tf_op | source)
XLA Modules:
  0.0 515.5 jit_solution(2411006129935054928)
XLA Ops:
  0.0 1.5 fusion.61
  1.5 0.7 copy-done.3
  2.2 0.4 copy-done.2
  2.5 0.3 fusion.14
  2.8 0.3 fusion.23
  3.1 0.6 copy-done.5
  3.7 0.3 fusion.60
  4.0 0.6 slice-done
  4.6 4.9 collective-permute-start
  9.5 0.7 copy-done.7
  10.2 2.0 collective-permute-done
  12.3 0.3 fusion.29
  12.6 0.7 copy-done.4
  13.3 32.6 %psum.112 = f32[2,128]{1,0:T(2,128)S(1)} all-reduce(f32[2,128]{1,0:T(2,128)S(1)} %fusion.9), channel_id=1, replica_groups=mesh['tm'=2,'cell'=16] {'cell'}, use_global_device_ids=true, to_apply=%region_1.2 | all-reduce | flops 256 | bytes 2048 | tf_op jit(solution)/shard_map/psum | solution.py:72
  46.0 0.4 fusion.6
  46.4 0.5 copy-done.1
  47.0 0.4 fusion.57
  47.4 29.5 %psum.113 = f32[2,128]{1,0:T(2,128)S(1)} all-reduce(f32[2,128]{1,0:T(2,128)S(1)} %get-tuple-element.85), channel_id=1, replica_groups=mesh['tm'=2,'cell'=16] {'cell'}, use_global_device_ids=true, to_apply=%region_3.4 | all-reduce | flops 256 | bytes 2048 | tf_op jit(solution)/shard_map/psum | solution.py:72
  77.0 0.4 fusion.33
  77.4 29.5 %psum.114 = f32[2,128]{1,0:T(2,128)S(1)} all-reduce(f32[2,128]{1,0:T(2,128)S(1)} %get-tuple-element.100), channel_id=1, replica_groups=mesh['tm'=2,'cell'=16] {'cell'}, use_global_device_ids=true, to_apply=%region_5.6 | all-reduce | flops 256 | bytes 2048 | tf_op jit(solution)/shard_map/psum | solution.py:72
  107.1 0.4 fusion.56
  107.5 29.5 %psum.115 = f32[2,128]{1,0:T(2,128)S(1)} all-reduce(f32[2,128]{1,0:T(2,128)S(1)} %get-tuple-element.81), channel_id=1, replica_groups=mesh['tm'=2,'cell'=16] {'cell'}, use_global_device_ids=true, to_apply=%region_7.8 | all-reduce | flops 256 | bytes 2048 | tf_op jit(solution)/shard_map/psum | solution.py:72
  137.0 0.1 multiply_add_fusion.12
  137.2 0.4 fusion.35
  137.6 29.5 %psum.116 = f32[2,128]{1,0:T(2,128)S(1)} all-reduce(f32[2,128]{1,0:T(2,128)S(1)} %get-tuple-element.103), channel_id=1, replica_groups=mesh['tm'=2,'cell'=16] {'cell'}, use_global_device_ids=true, to_apply=%region_9.10 | all-reduce | flops 256 | bytes 2048 | tf_op jit(solution)/shard_map/psum | solution.py:72
  167.2 0.4 fusion.55
  167.6 29.5 %psum.117 = f32[2,128]{1,0:T(2,128)S(1)} all-reduce(f32[2,128]{1,0:T(2,128)S(1)} %get-tuple-element.77), channel_id=1, replica_groups=mesh['tm'=2,'cell'=16] {'cell'}, use_global_device_ids=true, to_apply=%region_11.12 | all-reduce | flops 256 | bytes 2048 | tf_op jit(solution)/shard_map/psum | solution.py:72
  197.1 0.1 multiply_add_fusion.10
  197.3 0.4 fusion.37
  197.7 29.5 %psum.118 = f32[2,128]{1,0:T(2,128)S(1)} all-reduce(f32[2,128]{1,0:T(2,128)S(1)} %get-tuple-element.106), channel_id=1, replica_groups=mesh['tm'=2,'cell'=16] {'cell'}, use_global_device_ids=true, to_apply=%region_13.14 | all-reduce | flops 256 | bytes 2048 | tf_op jit(solution)/shard_map/psum | solution.py:72
  227.3 0.4 select_reduce_fusion.1
  227.8 29.5 %psum.119 = f32[2,128]{1,0:T(2,128)S(1)} all-reduce(f32[2,128]{1,0:T(2,128)S(1)} %get-tuple-element.108), channel_id=1, replica_groups=mesh['tm'=2,'cell'=16] {'cell'}, use_global_device_ids=true, to_apply=%region_15.16 | all-reduce | flops 256 | bytes 2048 | tf_op jit(solution)/shard_map/psum | solution.py:72
  257.3 0.1 multiply_add_fusion.8
  257.4 0.4 fusion.62
  258.0 0.3 fusion.20
  258.3 4.4 collective-permute-start.1
  262.7 2.8 collective-permute-done.1
  265.4 0.3 fusion.27
  265.8 29.5 %psum.120 = f32[2,128]{1,0:T(2,128)S(1)} all-reduce(f32[2,128]{1,0:T(2,128)S(1)} %fusion.8), channel_id=1, replica_groups=mesh['tm'=2,'cell'=16] {'cell'}, use_global_device_ids=true, to_apply=%region_17.18 | all-reduce | flops 256 | bytes 2048 | tf_op jit(solution)/shard_map/psum | solution.py:72
  295.3 0.4 fusion.4
  295.7 0.4 fusion.53
  296.2 29.5 %psum.121 = f32[2,128]{1,0:T(2,128)S(1)} all-reduce(f32[2,128]{1,0:T(2,128)S(1)} %get-tuple-element.63), channel_id=1, replica_groups=mesh['tm'=2,'cell'=16] {'cell'}, use_global_device_ids=true, to_apply=%region_19.20 | all-reduce | flops 256 | bytes 2048 | tf_op jit(solution)/shard_map/psum | solution.py:72
  325.8 0.4 fusion.34
  326.2 29.5 %psum.122 = f32[2,128]{1,0:T(2,128)S(1)} all-reduce(f32[2,128]{1,0:T(2,128)S(1)} %get-tuple-element.111), channel_id=1, replica_groups=mesh['tm'=2,'cell'=16] {'cell'}, use_global_device_ids=true, to_apply=%region_21.22 | all-reduce | flops 256 | bytes 2048 | tf_op jit(solution)/shard_map/psum | solution.py:72
  355.8 0.4 fusion.52
  356.3 29.5 %psum.123 = f32[2,128]{1,0:T(2,128)S(1)} all-reduce(f32[2,128]{1,0:T(2,128)S(1)} %get-tuple-element.53), channel_id=1, replica_groups=mesh['tm'=2,'cell'=16] {'cell'}, use_global_device_ids=true, to_apply=%region_23.24 | all-reduce | flops 256 | bytes 2048 | tf_op jit(solution)/shard_map/psum | solution.py:72
  385.8 0.1 multiply_add_fusion.4
  385.9 0.4 fusion.36
  386.4 29.5 %psum.124 = f32[2,128]{1,0:T(2,128)S(1)} all-reduce(f32[2,128]{1,0:T(2,128)S(1)} %get-tuple-element.114), channel_id=1, replica_groups=mesh['tm'=2,'cell'=16] {'cell'}, use_global_device_ids=true, to_apply=%region_25.26 | all-reduce | flops 256 | bytes 2048 | tf_op jit(solution)/shard_map/psum | solution.py:72
  416.0 0.4 fusion.51
  416.4 29.5 %psum.125 = f32[2,128]{1,0:T(2,128)S(1)} all-reduce(f32[2,128]{1,0:T(2,128)S(1)} %get-tuple-element.49), channel_id=1, replica_groups=mesh['tm'=2,'cell'=16] {'cell'}, use_global_device_ids=true, to_apply=%region_27.28 | all-reduce | flops 256 | bytes 2048 | tf_op jit(solution)/shard_map/psum | solution.py:72
  445.9 0.1 multiply_add_fusion.2
  446.1 0.4 fusion.38
  446.5 29.5 %psum.126 = f32[2,128]{1,0:T(2,128)S(1)} all-reduce(f32[2,128]{1,0:T(2,128)S(1)} %get-tuple-element.117), channel_id=1, replica_groups=mesh['tm'=2,'cell'=16] {'cell'}, use_global_device_ids=true, to_apply=%region_29.30 | all-reduce | flops 256 | bytes 2048 | tf_op jit(solution)/shard_map/psum | solution.py:72
  476.1 0.4 select_reduce_fusion
  476.6 29.5 %psum.127 = f32[2,128]{1,0:T(2,128)S(1)} all-reduce(f32[2,128]{1,0:T(2,128)S(1)} %get-tuple-element.119), channel_id=1, replica_groups=mesh['tm'=2,'cell'=16] {'cell'}, use_global_device_ids=true, to_apply=%region_31.32 | all-reduce | flops 256 | bytes 2048 | tf_op jit(solution)/shard_map/psum | solution.py:72
  506.0 0.1 multiply_add_fusion
  506.2 0.4 fusion.63
  506.7 0.3 fusion.18
  507.0 4.4 collective-permute-start.2
  511.5 2.7 collective-permute-done.2
  514.2 0.3 fusion.25
  514.5 0.3 fusion.16
  514.8 0.7 copy-done.8
  (56 shorter events, 1.7 us)
Async XLA Ops:
  0.0 47.0 %copy-start = (f32[2,2,128,128]{3,2,1,0:T(8,128)S(1)}, f32[2,2,128,128]{3,2,1,0:T(8,128)}, u32[]{:S(2)}) copy-start(f32[2,2,128,128]{3,2,1,0:T(8,128)} %param.9) | copy-start | bytes 786436
  1.5 0.7 copy-start.3
  1.5 1.0 copy-start.2
  2.8 0.9 copy-start.5
  3.7 0.9 slice-start
  4.6 7.6 %collective-permute-start = (f32[256,128]{1,0:T(8,128)S(1)}, f32[256,128]{1,0:T(8,128)S(1)}, u32[]{:S(2)}, u32[]{:S(2)}) collective-permute-start(f32[256,128]{1,0:T(8,128)S(1)} %fusion.13), channel_id=1, source_target_pairs={{0,16},{1,17},{2,18},{3,19},{4,20},{5,21},{6,22},{7,23},{8,24},{9,... | collective-permute-start | bytes 393224 | tf_op jit(solution)/shard_map/while/body/eval_jaxpr/ppermute | solution.py:13
  9.5 0.7 copy-start.7
  12.3 1.0 copy-start.4
  46.0 1.0 copy-start.1
  46.0 1.0 copy-start.6
  258.3 7.2 %collective-permute-start.1 = (f32[256,128]{1,0:T(8,128)S(1)}, f32[256,128]{1,0:T(8,128)S(1)}, u32[]{:S(2)}, u32[]{:S(2)}) collective-permute-start(f32[256,128]{1,0:T(8,128)S(1)} %fusion.11), channel_id=1, source_target_pairs={{0,16},{1,17},{2,18},{3,19},{4,20},{5,21},{6,22},{7,23},{8,24},{9,... | collective-permute-start | bytes 393224 | tf_op jit(solution)/shard_map/while/body/eval_jaxpr/ppermute | solution.py:13
  507.0 7.2 %collective-permute-start.2 = (f32[256,128]{1,0:T(8,128)S(1)}, f32[256,128]{1,0:T(8,128)S(1)}, u32[]{:S(2)}, u32[]{:S(2)}) collective-permute-start(f32[256,128]{1,0:T(8,128)S(1)} %fusion.12), channel_id=1, source_target_pairs={{0,16},{1,17},{2,18},{3,19},{4,20},{5,21},{6,22},{7,23},{8,24},{9,... | collective-permute-start | bytes 393224 | tf_op jit(solution)/shard_map/while/body/eval_jaxpr/ppermute | solution.py:13
  514.8 0.7 copy-start.8
where the time goes:
time: 516 us
  blocking collectives  475 us (92%)
  starting transfers between devices  13.7 us (3%)
  matrix products  11.5 us (2%)
  waiting for transfers between devices  7.54 us (1%)
    psum x16, blocking collectives, body(): average = lax.psum(jnp.sum(state, axis=1), 'cell') / total  475 us
    ppermute x3, starting transfers between devices, from_behind(): return lax.ppermute(block, axis, route)  13.7 us
  transfers between devices with their start and end apart: 3, of which 3 were waited for; matrix products, arithmetic and copies ran while one was open for 0% of the time, Pallas kernels for 0%

commit v1 on v0

--- a/solution.py
+++ b/solution.py
@@ -69,7 +69,7 @@
         starts = jnp.concatenate([incoming[None], finals[:-1]], axis=0)
         state = starts
         for substep in range(FINE_MAX):
-            average = lax.psum(jnp.sum(state, axis=1), "cell") / total
+            average = jnp.sum(lax.all_gather(jnp.sum(state, axis=1), "cell"), axis=0) / total
             moved = slices_mul(
                 state + source + mix_rate * (average[:, None, :] - state), fine_inverse
             )

time: 516 us -> 336 us (0.65)
  blocking collectives: 475 us -> 293 us
    psum x16 -> x0, blocking collectives: 475 us -> none  [body(): average = lax.psum(jnp.sum(state, axis=1), 'cell') / total]
    all_gather x0 -> x16, blocking collectives: none -> 293 us  [body(): lax.all_gather(jnp.sum(state, axis=1), 'cell')]
where the time goes in v1:
time: 336 us; the launch traced here: 335 us
  blocking collectives  293 us (87%)
  starting transfers between devices  13.7 us (4%)
  matrix products  11.5 us (3%)
  waiting for transfers between devices  8.5 us (3%)
  local copies, waits for them, and re-layouts  4.91 us (1%)
    all_gather x16, blocking collectives, body(): lax.all_gather(jnp.sum(state, axis=1), 'cell')  293 us
    ppermute x3, starting transfers between devices, from_behind(): return lax.ppermute(block, axis, route)  13.7 us
    dot_general x19, matrix products, slices_mul(): jnp.einsum('lgcs,lgst->lgct', shaped, matrices, precision=lax.Precision.H...  9.1 us
    ppermute x3, waiting for transfers between devices, from_behind(): return lax.ppermute(block, axis, route)  8.5 us
  transfers between devices with their start and end apart: 3, of which 3 were waited for; matrix products, arithmetic and copies ran while one was open for 0% of the time, Pallas kernels for 0%

profile of v1, /device:TPU:0, one launch (start us, length us, event | category | flops | bytes accessed | tf_op | source)
XLA Modules:
  0.0 335.2 jit_solution(1609604524278313381)
XLA Ops:
  0.0 1.5 fusion.61
  1.5 0.7 copy-done.3
  2.2 0.4 copy-done.2
  2.5 0.3 fusion.14
  2.8 0.3 fusion.23
  3.1 0.6 copy-done.5
  3.7 0.3 fusion.60
  4.0 0.6 slice-done
  4.6 4.9 %collective-permute-start = (f32[256,128]{1,0:T(8,128)S(1)}, f32[256,128]{1,0:T(8,128)S(1)}, u32[]{:S(2)}, u32[]{:S(2)}) collective-permute-start(f32[256,128]{1,0:T(8,128)S(1)} %fusion.13), channel_id=1, source_target_pairs={{0,16},{1,17},{2,18},{3,19},{4,20},{5,21},{6,22},{7,23},{8,24},{9,... | collective-permute-start | bytes 393224 | tf_op jit(solution)/shard_map/while/body/eval_jaxpr/ppermute | solution.py:13
  9.5 0.7 copy-done.7
  10.2 2.0 collective-permute-done
  12.3 0.3 fusion.29
  12.6 0.7 copy-done.4
  13.3 21.7 %all-gather.16 = f32[16,2,128]{2,1,0:T(2,128)S(1)} all-gather(f32[1,2,128]{2,1,0:T(2,128)S(1)} %bitcast.319), channel_id=2, replica_groups=mesh['tm'=2,'cell'=16] {'cell'}, dimensions={0}, use_global_device_ids=true | all-gather | bytes 17408 | tf_op jit(solution)/shard_map/all_gather | solution.py:72
  35.1 0.4 fusion.6
  35.5 0.5 copy-done.1
  36.0 0.4 fusion.57
  36.5 17.5 %all-gather.17 = f32[16,2,128]{2,1,0:T(2,128)S(1)} all-gather(f32[1,2,128]{2,1,0:T(2,128)S(1)} %bitcast.321), channel_id=3, replica_groups=mesh['tm'=2,'cell'=16] {'cell'}, dimensions={0}, use_global_device_ids=true | all-gather | bytes 17408 | tf_op jit(solution)/shard_map/all_gather | solution.py:72
  54.1 0.4 fusion.33
  54.5 18.8 %all-gather.18 = f32[16,2,128]{2,1,0:T(2,128)S(1)} all-gather(f32[1,2,128]{2,1,0:T(2,128)S(1)} %bitcast.313), channel_id=4, replica_groups=mesh['tm'=2,'cell'=16] {'cell'}, dimensions={0}, use_global_device_ids=true | all-gather | bytes 17408 | tf_op jit(solution)/shard_map/all_gather | solution.py:72
  73.5 0.4 fusion.56
  73.9 17.5 %all-gather.19 = f32[16,2,128]{2,1,0:T(2,128)S(1)} all-gather(f32[1,2,128]{2,1,0:T(2,128)S(1)} %bitcast.307), channel_id=5, replica_groups=mesh['tm'=2,'cell'=16] {'cell'}, dimensions={0}, use_global_device_ids=true | all-gather | bytes 17408 | tf_op jit(solution)/shard_map/all_gather | solution.py:72
  91.4 0.1 multiply_add_fusion.12
  91.6 0.4 fusion.35
  92.0 18.8 %all-gather.20 = f32[16,2,128]{2,1,0:T(2,128)S(1)} all-gather(f32[1,2,128]{2,1,0:T(2,128)S(1)} %bitcast.314), channel_id=6, replica_groups=mesh['tm'=2,'cell'=16] {'cell'}, dimensions={0}, use_global_device_ids=true | all-gather | bytes 17408 | tf_op jit(solution)/shard_map/all_gather | solution.py:72
  111.0 0.4 fusion.55
  111.4 17.5 %all-gather.21 = f32[16,2,128]{2,1,0:T(2,128)S(1)} all-gather(f32[1,2,128]{2,1,0:T(2,128)S(1)} %bitcast.308), channel_id=7, replica_groups=mesh['tm'=2,'cell'=16] {'cell'}, dimensions={0}, use_global_device_ids=true | all-gather | bytes 17408 | tf_op jit(solution)/shard_map/all_gather | solution.py:72
  128.9 0.1 multiply_add_fusion.10
  129.1 0.4 fusion.37
  129.5 18.8 %all-gather.22 = f32[16,2,128]{2,1,0:T(2,128)S(1)} all-gather(f32[1,2,128]{2,1,0:T(2,128)S(1)} %bitcast.315), channel_id=8, replica_groups=mesh['tm'=2,'cell'=16] {'cell'}, dimensions={0}, use_global_device_ids=true | all-gather | bytes 17408 | tf_op jit(solution)/shard_map/all_gather | solution.py:72
  148.5 0.4 select_reduce_fusion.1
  148.9 17.5 %all-gather.23 = f32[16,2,128]{2,1,0:T(2,128)S(1)} all-gather(f32[1,2,128]{2,1,0:T(2,128)S(1)} %bitcast.311), channel_id=9, replica_groups=mesh['tm'=2,'cell'=16] {'cell'}, dimensions={0}, use_global_device_ids=true | all-gather | bytes 17408 | tf_op jit(solution)/shard_map/all_gather | solution.py:72
  166.4 0.1 multiply_add_fusion.8
  166.6 0.4 fusion.62
  167.1 0.3 fusion.20
  167.4 4.4 %collective-permute-start.1 = (f32[256,128]{1,0:T(8,128)S(1)}, f32[256,128]{1,0:T(8,128)S(1)}, u32[]{:S(2)}, u32[]{:S(2)}) collective-permute-start(f32[256,128]{1,0:T(8,128)S(1)} %fusion.11), channel_id=1, source_target_pairs={{0,16},{1,17},{2,18},{3,19},{4,20},{5,21},{6,22},{7,23},{8,24},{9,... | collective-permute-start | bytes 393224 | tf_op jit(solution)/shard_map/while/body/eval_jaxpr/ppermute | solution.py:13
  171.8 3.2 collective-permute-done.1
  175.1 0.3 fusion.27
  175.4 18.8 %all-gather.24 = f32[16,2,128]{2,1,0:T(2,128)S(1)} all-gather(f32[1,2,128]{2,1,0:T(2,128)S(1)} %bitcast.320), channel_id=10, replica_groups=mesh['tm'=2,'cell'=16] {'cell'}, dimensions={0}, use_global_device_ids=true | all-gather | bytes 17408 | tf_op jit(solution)/shard_map/all_gather | solution.py:72
  194.3 0.4 fusion.4
  194.7 0.4 fusion.53
  195.1 17.5 %all-gather.25 = f32[16,2,128]{2,1,0:T(2,128)S(1)} all-gather(f32[1,2,128]{2,1,0:T(2,128)S(1)} %bitcast.322), channel_id=11, replica_groups=mesh['tm'=2,'cell'=16] {'cell'}, dimensions={0}, use_global_device_ids=true | all-gather | bytes 17408 | tf_op jit(solution)/shard_map/all_gather | solution.py:72
  212.8 0.4 fusion.34
  213.2 18.8 %all-gather.26 = f32[16,2,128]{2,1,0:T(2,128)S(1)} all-gather(f32[1,2,128]{2,1,0:T(2,128)S(1)} %bitcast.316), channel_id=12, replica_groups=mesh['tm'=2,'cell'=16] {'cell'}, dimensions={0}, use_global_device_ids=true | all-gather | bytes 17408 | tf_op jit(solution)/shard_map/all_gather | solution.py:72
  232.1 0.4 fusion.52
  232.6 17.5 %all-gather.27 = f32[16,2,128]{2,1,0:T(2,128)S(1)} all-gather(f32[1,2,128]{2,1,0:T(2,128)S(1)} %bitcast.309), channel_id=13, replica_groups=mesh['tm'=2,'cell'=16] {'cell'}, dimensions={0}, use_global_device_ids=true | all-gather | bytes 17408 | tf_op jit(solution)/shard_map/all_gather | solution.py:72
  250.1 0.1 multiply_add_fusion.4
  250.2 0.4 fusion.36
  250.7 19.0 %all-gather.28 = f32[16,2,128]{2,1,0:T(2,128)S(1)} all-gather(f32[1,2,128]{2,1,0:T(2,128)S(1)} %bitcast.317), channel_id=14, replica_groups=mesh['tm'=2,'cell'=16] {'cell'}, dimensions={0}, use_global_device_ids=true | all-gather | bytes 17408 | tf_op jit(solution)/shard_map/all_gather | solution.py:72
  269.8 0.4 fusion.51
  270.2 17.5 %all-gather.29 = f32[16,2,128]{2,1,0:T(2,128)S(1)} all-gather(f32[1,2,128]{2,1,0:T(2,128)S(1)} %bitcast.310), channel_id=15, replica_groups=mesh['tm'=2,'cell'=16] {'cell'}, dimensions={0}, use_global_device_ids=true | all-gather | bytes 17408 | tf_op jit(solution)/shard_map/all_gather | solution.py:72
  287.8 0.1 multiply_add_fusion.2
  287.9 0.4 fusion.38
  288.3 18.8 %all-gather.30 = f32[16,2,128]{2,1,0:T(2,128)S(1)} all-gather(f32[1,2,128]{2,1,0:T(2,128)S(1)} %bitcast.318), channel_id=16, replica_groups=mesh['tm'=2,'cell'=16] {'cell'}, dimensions={0}, use_global_device_ids=true | all-gather | bytes 17408 | tf_op jit(solution)/shard_map/all_gather | solution.py:72
  307.3 0.4 select_reduce_fusion
  307.7 17.5 %all-gather.31 = f32[16,2,128]{2,1,0:T(2,128)S(1)} all-gather(f32[1,2,128]{2,1,0:T(2,128)S(1)} %bitcast.312), channel_id=17, replica_groups=mesh['tm'=2,'cell'=16] {'cell'}, dimensions={0}, use_global_device_ids=true | all-gather | bytes 17408 | tf_op jit(solution)/shard_map/all_gather | solution.py:72
  325.2 0.1 multiply_add_fusion
  325.4 0.4 fusion.63
  325.9 0.3 fusion.18
  326.2 4.4 %collective-permute-start.2 = (f32[256,128]{1,0:T(8,128)S(1)}, f32[256,128]{1,0:T(8,128)S(1)}, u32[]{:S(2)}, u32[]{:S(2)}) collective-permute-start(f32[256,128]{1,0:T(8,128)S(1)} %fusion.12), channel_id=1, source_target_pairs={{0,16},{1,17},{2,18},{3,19},{4,20},{5,21},{6,22},{7,23},{8,24},{9,... | collective-permute-start | bytes 393224 | tf_op jit(solution)/shard_map/while/body/eval_jaxpr/ppermute | solution.py:13
  330.6 3.2 collective-permute-done.2
  333.9 0.3 fusion.25
  334.2 0.3 fusion.16
  334.5 0.7 copy-done.8
  (72 shorter events, 2.1 us)
Async XLA Ops:
  0.0 36.0 %copy-start = (f32[2,2,128,128]{3,2,1,0:T(8,128)S(1)}, f32[2,2,128,128]{3,2,1,0:T(8,128)}, u32[]{:S(2)}) copy-start(f32[2,2,128,128]{3,2,1,0:T(8,128)} %param.9) | copy-start | bytes 786436
  1.5 0.7 copy-start.3
  1.5 1.0 copy-start.2
  2.8 0.9 copy-start.5
  3.7 0.9 slice-start
  4.6 7.6 %collective-permute-start = (f32[256,128]{1,0:T(8,128)S(1)}, f32[256,128]{1,0:T(8,128)S(1)}, u32[]{:S(2)}, u32[]{:S(2)}) collective-permute-start(f32[256,128]{1,0:T(8,128)S(1)} %fusion.13), channel_id=1, source_target_pairs={{0,16},{1,17},{2,18},{3,19},{4,20},{5,21},{6,22},{7,23},{8,24},{9,... | collective-permute-start | bytes 393224 | tf_op jit(solution)/shard_map/while/body/eval_jaxpr/ppermute | solution.py:13
  9.5 0.7 copy-start.7
  12.3 1.0 copy-start.4
  35.0 0.9 copy-start.1
  35.0 0.9 copy-start.6
  167.4 7.6 %collective-permute-start.1 = (f32[256,128]{1,0:T(8,128)S(1)}, f32[256,128]{1,0:T(8,128)S(1)}, u32[]{:S(2)}, u32[]{:S(2)}) collective-permute-start(f32[256,128]{1,0:T(8,128)S(1)} %fusion.11), channel_id=1, source_target_pairs={{0,16},{1,17},{2,18},{3,19},{4,20},{5,21},{6,22},{7,23},{8,24},{9,... | collective-permute-start | bytes 393224 | tf_op jit(solution)/shard_map/while/body/eval_jaxpr/ppermute | solution.py:13
  326.2 7.6 %collective-permute-start.2 = (f32[256,128]{1,0:T(8,128)S(1)}, f32[256,128]{1,0:T(8,128)S(1)}, u32[]{:S(2)}, u32[]{:S(2)}) collective-permute-start(f32[256,128]{1,0:T(8,128)S(1)} %fusion.12), channel_id=1, source_target_pairs={{0,16},{1,17},{2,18},{3,19},{4,20},{5,21},{6,22},{7,23},{8,24},{9,... | collective-permute-start | bytes 393224 | tf_op jit(solution)/shard_map/while/body/eval_jaxpr/ppermute | solution.py:13
  334.5 0.7 copy-start.8
